TPU v7x, 32 devices: a whole 2x2x4 slice. The times are simulated.
32 devices in a mesh: space: 4 (over y, x), orb: 8 (over z, core).
Axes of the slice: x: 2, y: 2, z: 4, core: 2. Of those that a mesh axis runs over, the one named last changes fastest.
Arguments:
- orbitals: float32 [16, 16, 32, 1024], P('space', None, None, 'orb'), may hold values from -6 to 6
- potential: float32 [16, 16, 32], P('space'), may hold values from 0 to 2
Outputs:
- updated: float32 [16, 16, 32, 1024], P('space', None, None, 'orb')
All inputs are finite; a program needn't handle non-finite values.
Results may differ from a plain program's by a relative error of at most 0.00007.
Values sent between devices are 32-bit elements; how exact they have to be, the bound alone decides.
A program may use at most 64 MiB of HBM per device.

v0:
```python
import jax
import jax.numpy as jnp
from jax import lax
from jax.sharding import PartitionSpec as P

PANEL = 512
DEGREE = 4


STENCIL = (-205.0 / 72.0, 8.0 / 5.0, -1.0 / 5.0, 8.0 / 315.0, -1.0 / 560.0)
SHIFT_MID = 7.25
HALF_WIDTH = 4.75


def padded_2(shard, sides, width):
    for axis, dim in sides:
        count, length = (lax.axis_size(axis), shard.shape[dim])
        up = [(i, (i + 1) % count) for i in range(count)]
        down = [(j, i) for i, j in up]
        last = lax.slice_in_dim(shard, length - width, length, axis=dim)
        leading = lax.slice_in_dim(shard, 0, width, axis=dim)
        before = lax.ppermute(last, axis, up)
        after = lax.ppermute(leading, axis, down)
        shard = jnp.concatenate([before, shard, after], axis=dim)
    return shard


def hamilton(field, potential):
    planes = field.shape[0]
    padded = padded_2(field, (("space", 0),), 4)
    laplace = 3.0 * STENCIL[0] * field
    for offset in range(1, 5):
        upper = padded[4 + offset : 4 + offset + planes]
        below = padded[4 - offset : 4 - offset + planes]
        laplace = laplace + STENCIL[offset] * (upper + below)
    for axis in (1, 2):
        for offset in range(1, 5):
            laplace = laplace + STENCIL[offset] * (
                jnp.roll(field, offset, axis) + jnp.roll(field, -offset, axis)
            )
    return -0.5 * laplace + potential[..., None] * field


def chebyshev(block, potential):
    before = block
    current = (hamilton(block, potential) - SHIFT_MID * block) / HALF_WIDTH
    for order in range(DEGREE - 1):
        following = 2.0 * (hamilton(current, potential) - SHIFT_MID * current) / HALF_WIDTH - before
        before, current = (current, following)
    return current


def per_device(orbitals, potential):
    highest = lax.Precision.HIGHEST
    filtered = chebyshev(orbitals, potential)
    planes, rows_y, rows_z, columns = filtered.shape
    local_points = planes * rows_y * rows_z
    points = local_points * lax.axis_size("space")
    panel_dev = PANEL // lax.axis_size("orb")
    flat = filtered.reshape(local_points, columns)
    panel_own = flat[:, :panel_dev]
    trailing = flat[:, panel_dev:]
    panel = lax.all_gather(panel_own, "orb", axis=1, tiled=True)
    coupling_part = jnp.dot(panel.T, trailing, precision=highest)
    gram_part = jnp.dot(panel.T, panel, precision=highest)
    gram_full, coupling = lax.psum((gram_part, coupling_part), "space")
    gram_full = gram_full / points
    coupling = coupling / points
    lower_factor = jnp.linalg.cholesky(gram_full)
    identity = jnp.eye(PANEL, dtype=jnp.float32)
    inverse = lax.linalg.triangular_solve(lower_factor, identity, left_side=True, lower=True)
    start = lax.axis_index("orb") * panel_dev
    own_rows = lax.dynamic_slice_in_dim(inverse, start, panel_dev, 0)
    ortho_own = jnp.dot(panel, own_rows.T, precision=highest)
    middle = jnp.dot(inverse, coupling, precision=highest)
    project = jnp.dot(inverse.T, middle, precision=highest)
    trailing_new = trailing - jnp.dot(panel, project, precision=highest)
    joined = jnp.concatenate([ortho_own, trailing_new], axis=1)
    return joined.reshape(planes, rows_y, rows_z, columns)


def solution(mesh):
    placed = (P("space", None, None, "orb"), P("space", None, None))
    return jax.shard_map(
        per_device,
        mesh=mesh,
        in_specs=placed,
        out_specs=P("space", None, None, "orb"),
        check_vma=False,
    )
```

profile of v0, /device:TPU:0, one launch (start us, length us, event | category | flops | bytes accessed | tf_op | source)
XLA Modules:
  0.0 514.7 jit_solution(1693416008679827727)
XLA Ops:
  6.5 3.0 collective-permute-start.1
  21.2 13.6 %collective-permute-done.1 = f32[4,16,32,128]{3,2,1,0:T(8,128)S(1)} collective-permute-done((f32[4,16,32,128]{3,2,1,0:T(8,128)}, f32[4,16,32,128]{3,2,1,0:T(8,128)S(1)}, u32[]{:S(2)}, u32[]{:S(2)}) %collective-permute-start.1) | collective-permute-done | bytes 1048608 | tf_op jit(solution)/shard_map/ppermute | solution.py:22
  35.0 21.6 %collective-permute-done = f32[4,16,32,128]{3,2,1,0:T(8,128)S(1)} collective-permute-done((f32[4,16,32,128]{3,2,1,0:T(8,128)}, f32[4,16,32,128]{3,2,1,0:T(8,128)S(1)}, u32[]{:S(2)}, u32[]{:S(2)}) %collective-permute-start) | collective-permute-done | bytes 1048608 | tf_op jit(solution)/shard_map/ppermute | solution.py:23
  56.6 5.3 %broadcast_multiply_fusion.1 = (f32[4,16,32,128]{3,2,1,0:T(8,128)S(1)}, f32[4,16,32,128]{3,2,1,0:T(8,128)S(1)}) fusion(f32[4,16,32,128]{3,2,1,0:T(8,128)S(1)} %copy-done, f32[4,16,32]{2,1,0:T(8,128)S(1)} %copy-done.12, f32[4,16,4,128]{3,2,1,0:T(4,128)} %get-tuple-element.156, f32[4,16,28,128]{3,2,1,0:T(8,128)S(1)} %get-tuple-element.158, ...), kind=kLoop, calls=%fused_computation.211 | loop fusion | flops 15466496 | bytes 28319744 | tf_op jit(solution)/shard_map/div | solution.py:46
  72.9 22.7 %collective-permute-done.2 = f32[4,16,32,128]{3,2,1,0:T(8,128)S(1)} collective-permute-done((f32[4,16,32,128]{3,2,1,0:T(8,128)S(1)}, f32[4,16,32,128]{3,2,1,0:T(8,128)S(1)}, u32[]{:S(2)}, u32[]{:S(2)}) %collective-permute-start.2) | collective-permute-done | bytes 1048608 | tf_op jit(solution)/shard_map/ppermute | solution.py:23
  95.6 20.6 %collective-permute-done.3 = f32[4,16,32,128]{3,2,1,0:T(8,128)S(1)} collective-permute-done((f32[4,16,32,128]{3,2,1,0:T(8,128)S(1)}, f32[4,16,32,128]{3,2,1,0:T(8,128)S(1)}, u32[]{:S(2)}, u32[]{:S(2)}) %collective-permute-start.3) | collective-permute-done | bytes 1048608 | tf_op jit(solution)/shard_map/ppermute | solution.py:22
  117.2 6.9 %multiply_subtract_fusion.2 = f32[4,16,32,128]{3,2,1,0:T(8,128)S(1)} fusion(f32[4,16,32,128]{3,2,1,0:T(8,128)S(1)} %copy-done, f32[4,16,32,128]{3,2,1,0:T(8,128)S(1)} %get-tuple-element.24, f32[4,16,4,128]{3,2,1,0:T(4,128)} %get-tuple-element.122, f32[4,16,28,128]{3,2,1,0:T(8,128)S(1)} %get-tuple-element.124, f32[4,16,28,128]{3,2,1,0:T(8,128)S(1)} %get-tuple-element.123, ...), kind=kLoop, calls=%fused_computation.201 | loop fusion | flops 17301504 | bytes 23076864 | tf_op jit(solution)/shard_map/sub | solution.py:48
  126.0 2.3 collective-permute-start.4
  135.1 17.0 %collective-permute-done.4 = f32[4,16,32,128]{3,2,1,0:T(8,128)S(1)} collective-permute-done((f32[4,16,32,128]{3,2,1,0:T(8,128)S(1)}, f32[4,16,32,128]{3,2,1,0:T(8,128)S(1)}, u32[]{:S(2)}, u32[]{:S(2)}) %collective-permute-start.4) | collective-permute-done | bytes 1048608 | tf_op jit(solution)/shard_map/ppermute | solution.py:23
  152.1 20.4 %collective-permute-done.5 = f32[4,16,32,128]{3,2,1,0:T(8,128)S(1)} collective-permute-done((f32[4,16,32,128]{3,2,1,0:T(8,128)S(1)}, f32[4,16,32,128]{3,2,1,0:T(8,128)S(1)}, u32[]{:S(2)}, u32[]{:S(2)}) %collective-permute-start.5) | collective-permute-done | bytes 1048608 | tf_op jit(solution)/shard_map/ppermute | solution.py:22
  173.5 6.9 %multiply_subtract_fusion.1 = f32[4,16,32,128]{3,2,1,0:T(8,128)S(1)} fusion(f32[4,16,32,128]{3,2,1,0:T(8,128)S(1)} %multiply_subtract_fusion.2, f32[4,16,4,128]{3,2,1,0:T(4,128)} %get-tuple-element.90, f32[4,16,28,128]{3,2,1,0:T(8,128)S(1)} %get-tuple-element.92, f32[4,16,28,128]{3,2,1,0:T(8,128)S(1)} %get-tuple-element.91, ...), kind=kLoop, calls=%fused_computation.200 | loop fusion | flops 17563648 | bytes 22028288 | tf_op jit(solution)/shard_map/sub | solution.py:48
  190.4 18.2 %collective-permute-done.6 = f32[4,16,32,128]{3,2,1,0:T(8,128)S(1)} collective-permute-done((f32[4,16,32,128]{3,2,1,0:T(8,128)S(1)}, f32[4,16,32,128]{3,2,1,0:T(8,128)S(1)}, u32[]{:S(2)}, u32[]{:S(2)}) %collective-permute-start.6) | collective-permute-done | bytes 1048608 | tf_op jit(solution)/shard_map/ppermute | solution.py:23
  208.7 19.4 %collective-permute-done.7 = f32[4,16,32,128]{3,2,1,0:T(8,128)S(1)} collective-permute-done((f32[4,16,32,128]{3,2,1,0:T(8,128)S(1)}, f32[4,16,32,128]{3,2,1,0:T(8,128)S(1)}, u32[]{:S(2)}, u32[]{:S(2)}) %collective-permute-start.7) | collective-permute-done | bytes 1048608 | tf_op jit(solution)/shard_map/ppermute | solution.py:22
  229.1 6.8 %multiply_subtract_fusion = f32[4,16,32,128]{3,2,1,0:T(8,128)S(1)} fusion(f32[4,16,32,128]{3,2,1,0:T(8,128)S(1)} %multiply_subtract_fusion.2, f32[4,16,32,128]{3,2,1,0:T(8,128)S(1)} %multiply_subtract_fusion.1, f32[4,16,4,128]{3,2,1,0:T(4,128)} %get-tuple-element.58, f32[4,16,28,128]{3,2,1,0:T(8,128)S(1)} %get-tuple-element.60, ...), kind=kLoop, calls=%fused_computation.199 | loop fusion | flops 17301504 | bytes 22028288 | tf_op jit(solution)/shard_map/sub | solution.py:48
  237.5 47.5 %all-gather.2.cloned.1.call-done = f32[2048,512]{0,1:T(8,128)} async-done(((f32[2048,64]{0,1:T(8,128)}), f32[2048,512]{0,1:T(8,128)}) %all-gather.2.cloned.1.call-update) | async-done | bytes 4194320 | tf_op jit(solution)/shard_map/all_gather | solution.py:63
  285.0 10.7 %fusion.224 = f32[512,512]{0,1:T(8,128)} fusion(f32[2048,512]{0,1:T(8,128)} %all-gather.2.cloned.1.call-done), kind=kOutput, calls=%fused_computation.337 | convolution fusion | flops 6442450944 | bytes 5242880 | tf_op jit(solution)/shard_map/dot_general | solution.py:65
  295.7 4.9 fusion.154
  303.0 51.0 %all-reduce.4.cloned.1.call-done = (f32[512,64]{0,1:T(8,128)}, f32[512,512]{0,1:T(8,128)}) async-done(((f32[512,64]{0,1:T(8,128)}, f32[512,512]{0,1:T(8,128)}), (f32[512,64]{0,1:T(8,128)}, f32[512,512]{0,1:T(8,128)})) %all-reduce.4.cloned.1.call-update) | async-done | bytes 1179664 | tf_op jit(solution)/shard_map/psum | solution.py:66
  356.0 11.7 %cholesky.104 = f32[128,128]{1,0:T(8,128)S(1)} custom-call(f32[128,128]{1,0:T(8,128)S(1)} %cholesky.266), custom_call_target="Cholesky" | custom-call | tf_op jit(solution)/shard_map/jit(cholesky)/cholesky | solution.py:69
  367.9 9.8 %custom-call.30 = f32[1,128,128]{1,2,0:T(8,128)S(1)} custom-call(f32[1,128,128]{2,1,0:T(8,128)S(1)} %get-tuple-element.168), custom_call_target="InvertDiagBlocksLowerTriangular" | custom-call | tf_op jit(solution)/shard_map/jit(cholesky)/cholesky | solution.py:69
  378.4 11.9 %cholesky.217 = f32[128,128]{1,0:T(8,128)S(1)} custom-call(f32[128,128]{1,0:T(8,128)S(1)} %cholesky.270), custom_call_target="Cholesky" | custom-call | tf_op jit(solution)/shard_map/jit(cholesky)/cholesky | solution.py:69
  390.3 9.8 %custom-call.31 = f32[1,128,128]{1,2,0:T(8,128)S(1)} custom-call(f32[1,128,128]{2,1,0:T(8,128)S(1)} %get-tuple-element.165), custom_call_target="InvertDiagBlocksLowerTriangular" | custom-call | tf_op jit(solution)/shard_map/jit(cholesky)/cholesky | solution.py:69
  400.8 12.3 %cholesky.238 = f32[128,128]{1,0:T(8,128)} custom-call(f32[128,128]{1,0:T(8,128)S(1)} %cholesky.275), custom_call_target="Cholesky" | custom-call | tf_op jit(solution)/shard_map/jit(cholesky)/cholesky | solution.py:69
  415.4 11.3 %custom-call.32 = f32[1,128,128]{1,2,0:T(8,128)} custom-call(f32[1,128,128]{2,1,0:T(8,128)} %get-tuple-element.162), custom_call_target="InvertDiagBlocksLowerTriangular" | custom-call | tf_op jit(solution)/shard_map/jit(cholesky)/cholesky | solution.py:69
  428.1 11.9 %cholesky.255 = f32[128,128]{1,0:T(8,128)S(1)} custom-call(f32[128,128]{1,0:T(8,128)S(1)} %convolution_subtract_fusion.6), custom_call_target="Cholesky" | custom-call | tf_op jit(solution)/shard_map/jit(cholesky)/cholesky | solution.py:69
  444.2 10.8 %while.1 = (s32[]{:T(128)}, f32[512,512]{1,0:T(8,128)S(1)}, s32[4,2]{0,1:T(2,128)S(1)}, f32[4,128,128]{2,1,0:T(8,128)}, s32[]{:T(128)}) while((s32[]{:T(128)}, f32[512,512]{1,0:T(8,128)S(1)}, s32[4,2]{0,1:T(2,128)S(1)}, f32[4,128,128]{2,1,0:T(8,128)}, s32[]{:T(128)}) %tuple.94), condition=%wide.while_cond, body=%wide.while_body.sunk | while | flops 2 | bytes 132705 | solution.py:71
  444.9 2.0 bitcast_dynamic-update-slice_fusion.2
  450.2 2.0 bitcast_dynamic-update-slice_fusion.2
  452.9 2.0 bitcast_dynamic-update-slice_fusion.2
  455.0 40.1 %custom-call.33 = f32[4,128,128]{1,2,0:T(8,128)S(1)} custom-call(f32[4,128,128]{2,1,0:T(8,128)} %get-tuple-element.12), custom_call_target="InvertDiagBlocksLowerTriangular" | custom-call | tf_op jit(solution)/shard_map/triangular_solve | solution.py:71
  500.4 2.8 fusion.138
  503.2 2.8 convolution_subtract_fusion
  (158 shorter events, 68.2 us)
Async XLA Ops:
  6.5 5.8 %copy-start = (f32[4,16,32,128]{3,2,1,0:T(8,128)S(1)}, f32[4,16,32,128]{3,2,1,0:T(8,128)}, u32[]{:S(2)}) copy-start(f32[4,16,32,128]{3,2,1,0:T(8,128)} %param.2) | copy-start | bytes 3145732
  6.5 278.4 %all-gather.2.cloned.1.call-start = ((), (), s32[]{:S(2)}) async-start(), calls=%async_computation | async-start | bytes 4718592 | tf_op jit(solution)/shard_map/all_gather | solution.py:63
  6.5 28.2 %collective-permute-start.1 = (f32[4,16,32,128]{3,2,1,0:T(8,128)}, f32[4,16,32,128]{3,2,1,0:T(8,128)S(1)}, u32[]{:S(2)}, u32[]{:S(2)}) collective-permute-start(f32[4,16,32,128]{3,2,1,0:T(8,128)} %param.2), channel_id=1, source_target_pairs={{0,8},{8,16},{16,24},{24,0},{1,9},{9,17},{17,25},{25,1},{2,10},{10... | collective-permute-start | bytes 3145736 | tf_op jit(solution)/shard_map/ppermute | solution.py:22
  9.5 47.0 %collective-permute-start = (f32[4,16,32,128]{3,2,1,0:T(8,128)}, f32[4,16,32,128]{3,2,1,0:T(8,128)S(1)}, u32[]{:S(2)}, u32[]{:S(2)}) collective-permute-start(f32[4,16,32,128]{3,2,1,0:T(8,128)} %param.2), channel_id=1, source_target_pairs={{8,0},{16,8},{24,16},{0,24},{9,1},{17,9},{25,17},{1,25},{10,2},{18... | collective-permute-start | bytes 3145736 | tf_op jit(solution)/shard_map/ppermute | solution.py:23
  16.4 4.3 copy-start.12
  69.5 26.0 %collective-permute-start.2 = (f32[4,16,32,128]{3,2,1,0:T(8,128)S(1)}, f32[4,16,32,128]{3,2,1,0:T(8,128)S(1)}, u32[]{:S(2)}, u32[]{:S(2)}) collective-permute-start(f32[4,16,32,128]{3,2,1,0:T(8,128)S(1)} %get-tuple-element.23), channel_id=1, source_target_pairs={{8,0},{16,8},{24,16},{0,24},{9,1},{17,9},{25,17},{1,25},{10,2},{18... | collective-permute-start | bytes 3145736 | tf_op jit(solution)/shard_map/ppermute | solution.py:23
  71.0 45.2 %collective-permute-start.3 = (f32[4,16,32,128]{3,2,1,0:T(8,128)S(1)}, f32[4,16,32,128]{3,2,1,0:T(8,128)S(1)}, u32[]{:S(2)}, u32[]{:S(2)}) collective-permute-start(f32[4,16,32,128]{3,2,1,0:T(8,128)S(1)} %get-tuple-element.23), channel_id=1, source_target_pairs={{0,8},{8,16},{16,24},{24,0},{1,9},{9,17},{17,25},{25,1},{2,10},{10... | collective-permute-start | bytes 3145736 | tf_op jit(solution)/shard_map/ppermute | solution.py:22
  95.6 20.6 %copy-start.10 = (f32[4,16,32,128]{3,2,1,0:T(8,128)}, f32[4,16,32,128]{3,2,1,0:T(8,128)S(1)}, u32[]{:S(2)}) copy-start(f32[4,16,32,128]{3,2,1,0:T(8,128)S(1)} %collective-permute-done.2) | copy-start | bytes 3145732
  116.2 1.0 copy-start.11
  126.0 26.0 %collective-permute-start.4 = (f32[4,16,32,128]{3,2,1,0:T(8,128)S(1)}, f32[4,16,32,128]{3,2,1,0:T(8,128)S(1)}, u32[]{:S(2)}, u32[]{:S(2)}) collective-permute-start(f32[4,16,32,128]{3,2,1,0:T(8,128)S(1)} %multiply_subtract_fusion.2), channel_id=1, source_target_pairs={{8,0},{16,8},{24,16},{0,24},{9,1},{17,9},{25,17},{1,25},{10,2},{18... | collective-permute-start | bytes 3145736 | tf_op jit(solution)/shard_map/ppermute | solution.py:23
  128.3 44.2 %collective-permute-start.5 = (f32[4,16,32,128]{3,2,1,0:T(8,128)S(1)}, f32[4,16,32,128]{3,2,1,0:T(8,128)S(1)}, u32[]{:S(2)}, u32[]{:S(2)}) collective-permute-start(f32[4,16,32,128]{3,2,1,0:T(8,128)S(1)} %multiply_subtract_fusion.2), channel_id=1, source_target_pairs={{0,8},{8,16},{16,24},{24,0},{1,9},{9,17},{17,25},{25,1},{2,10},{10... | collective-permute-start | bytes 3145736 | tf_op jit(solution)/shard_map/ppermute | solution.py:22
  152.1 20.4 %copy-start.7 = (f32[4,16,32,128]{3,2,1,0:T(8,128)}, f32[4,16,32,128]{3,2,1,0:T(8,128)S(1)}, u32[]{:S(2)}) copy-start(f32[4,16,32,128]{3,2,1,0:T(8,128)S(1)} %collective-permute-done.4) | copy-start | bytes 3145732
  172.5 1.0 copy-start.9
  182.6 26.0 %collective-permute-start.6 = (f32[4,16,32,128]{3,2,1,0:T(8,128)S(1)}, f32[4,16,32,128]{3,2,1,0:T(8,128)S(1)}, u32[]{:S(2)}, u32[]{:S(2)}) collective-permute-start(f32[4,16,32,128]{3,2,1,0:T(8,128)S(1)} %multiply_subtract_fusion.1), channel_id=1, source_target_pairs={{8,0},{16,8},{24,16},{0,24},{9,1},{17,9},{25,17},{1,25},{10,2},{18... | collective-permute-start | bytes 3145736 | tf_op jit(solution)/shard_map/ppermute | solution.py:23
  184.1 44.0 %collective-permute-start.7 = (f32[4,16,32,128]{3,2,1,0:T(8,128)S(1)}, f32[4,16,32,128]{3,2,1,0:T(8,128)S(1)}, u32[]{:S(2)}, u32[]{:S(2)}) collective-permute-start(f32[4,16,32,128]{3,2,1,0:T(8,128)S(1)} %multiply_subtract_fusion.1), channel_id=1, source_target_pairs={{0,8},{8,16},{16,24},{24,0},{1,9},{9,17},{17,25},{25,1},{2,10},{10... | collective-permute-start | bytes 3145736 | tf_op jit(solution)/shard_map/ppermute | solution.py:22
  190.2 38.9 %copy-start.13 = (f32[4,16,32]{2,1,0:T(8,128)S(1)}, f32[4,16,32]{2,1,0:T(8,128)}, u32[]{:S(2)}) copy-start(f32[4,16,32]{2,1,0:T(8,128)} %param.3) | copy-start | bytes 24580
  208.7 19.4 %copy-start.6 = (f32[4,16,32,128]{3,2,1,0:T(8,128)}, f32[4,16,32,128]{3,2,1,0:T(8,128)S(1)}, u32[]{:S(2)}) copy-start(f32[4,16,32,128]{3,2,1,0:T(8,128)S(1)} %collective-permute-done.6) | copy-start | bytes 3145732
  228.1 1.0 copy-start.8
  237.4 116.6 %all-reduce.4.cloned.1.call-start = ((), (), s32[]{:S(2)}) async-start(), calls=%async_computation.1 | async-start | bytes 2359296 | tf_op jit(solution)/shard_map/psum | solution.py:66
  285.0 10.7 %copy-start.1 = (f32[2048,512]{0,1:T(8,128)S(1)}, f32[2048,512]{0,1:T(8,128)}, u32[]{:S(2)}) copy-start(f32[2048,512]{0,1:T(8,128)} %all-gather.2.cloned.1.call-done) | copy-start | bytes 12582916
  354.0 1.8 copy-start.3
  413.1 82.3 %copy-start.4 = (f32[512,512]{1,0:T(8,128)S(1)}, f32[512,512]{1,0:T(8,128)}, u32[]{:S(2)}) copy-start(f32[512,512]{1,0:T(8,128)} %fusion.125) | copy-start | bytes 3145732
  497.1 1.2 copy-start.14
  498.2 2.2 copy-start.2
  500.4 2.9 copy-start.5
Sparse Core Ops, SparseCore 0:
  237.5 47.3 all-gather.1
  300.8 53.1 all-reduce.3
where the time goes:
time: 522 us; the launch traced here: 515 us
  waiting for transfers between devices  252 us (48%)
  other arithmetic  152 us (29%)
  local copies, waits for them, and re-layouts  54.5 us (10%)
  matrix products  29 us (6%)
  between operations  17 us (3%)
  starting transfers between devices  10.5 us (2%)
    another operation x14, other arithmetic, per_device(): lower_factor = jnp.linalg.cholesky(gram_full)  82.5 us
    ppermute x4, waiting for transfers between devices, padded_2(): after = lax.ppermute(leading, axis, down)  79.4 us
    ppermute x4, waiting for transfers between devices, padded_2(): before = lax.ppermute(last, axis, up)  74 us
    psum x1, waiting for transfers between devices, per_device(): gram_full, coupling = lax.psum((gram_part, coupling_part), 'space')  51 us
    all_gather x1, waiting for transfers between devices, per_device(): panel = lax.all_gather(panel_own, 'orb', axis=1, tiled=True)  47.5 us
    another operation x4, other arithmetic, per_device(): lax.linalg.triangular_solve(lower_factor, identity, left_side=True, lower...  40.3 us
    slice x64, local copies, waits for them, and re-layouts, hamilton(): jnp.roll(field, offset, axis) + jnp.roll(field, -offset, axis)  35.9 us
    sub x3, other arithmetic, chebyshev(): 2.0 * (hamilton(current, potential) - SHIFT_MID * current) / HALF_WIDTH  20.7 us
  transfers between devices with their start and end apart: 10, of which 10 were waited for; matrix products, arithmetic and copies ran while one was open for 5% of the time, Pallas kernels for 0%

commit v1 on v0

v1 whole, which is shorter than its diff:
```python
import functools

import jax
import jax.numpy as jnp
from jax import lax
from jax.experimental import pallas as pl
from jax.experimental.pallas import tpu as pltpu
from jax.sharding import PartitionSpec as P

PANEL = 512
DEGREE = 4

STENCIL = (-205.0 / 72.0, 8.0 / 5.0, -1.0 / 5.0, 8.0 / 315.0, -1.0 / 560.0)
SHIFT_MID = 7.25
HALF_WIDTH = 4.75
LANES = 128
REACH = 4
MESH = pl.DeviceIdType.MESH
HIGHEST = lax.Precision.HIGHEST


def dot(a, b, dims):
    return lax.dot_general(
        a, b, ((dims[:1], dims[1:]), ((), ())), precision=HIGHEST, preferred_element_type=jnp.float32
    )


def regroup(load, store, count, rows):
    width = LANES // count
    step = min(rows, max(8, 128 // count))
    group = lax.broadcasted_iota(jnp.int32, (step, LANES), 1) // width

    def body(block, carry):
        here = pl.ds(pl.multiple_of(block * step, step), step)
        parts = [load(r, here) for r in range(count)]
        for j in range(count):
            out = None
            for r in range(count):
                turn = ((r - j) * width) % LANES
                piece = pltpu.roll(parts[r], turn, 1) if turn else parts[r]
                out = piece if out is None else jnp.where(group == r, piece, out)
            store(j, here, out)
        return carry

    lax.fori_loop(0, rows // step, body, 0)


def exchange(slots, here, send_sem, recv_sem, send, land):
    copies = []
    for hop in range(1, slots):
        there = lax.rem(here + hop, slots)
        copy = pltpu.make_async_remote_copy(
            src_ref=send(there),
            dst_ref=land.at[here],
            send_sem=send_sem.at[hop],
            recv_sem=recv_sem.at[hop],
            device_id={"space": there},
            device_id_type=MESH,
        )
        copy.start()
        copies.append(copy)
    return copies


def wait_exchange(slots, here, send_sem, recv_sem, send, land):
    for hop in range(1, slots):
        there = lax.rem(here + hop, slots)
        source = lax.rem(here + slots - hop, slots)
        pltpu.make_async_remote_copy(
            src_ref=send(there),
            dst_ref=land.at[source],
            send_sem=send_sem.at[hop],
            recv_sem=recv_sem.at[hop],
            device_id={"space": there},
            device_id_type=MESH,
        ).wait()


def gather_orb(count, me, buf, send_sem, recv_sem, side_send, side_recv):
    chips = count // 2
    chip, core = me // 2, lax.rem(me, 2)
    partner = chip * 2 + (1 - core)

    def along(origin, to, way, step):
        slot = buf.at[origin * 2 + core]
        return pltpu.make_async_remote_copy(
            src_ref=slot,
            dst_ref=slot,
            send_sem=send_sem.at[way, step],
            recv_sem=recv_sem.at[way, step],
            device_id={"orb": to * 2 + core},
            device_id_type=MESH,
        )

    def across(origin, side, index):
        slot = buf.at[origin * 2 + side]
        return pltpu.make_async_remote_copy(
            src_ref=slot,
            dst_ref=slot,
            send_sem=side_send.at[index],
            recv_sem=side_recv.at[index],
            device_id={"orb": partner},
            device_id_type=MESH,
        )

    steps = chips - 1
    for step in range(steps):
        @pl.when((chip - step >= 0) & (chip + 1 < chips))
        def _():
            along(chip - step, chip + 1, 0, step).start()

        @pl.when((chip + step < chips) & (chip - 1 >= 0))
        def _():
            along(chip + step, chip - 1, 1, step).start()

        if step == 0:
            across(chip, core, 0).start()

        @pl.when(chip - 1 - step >= 0)
        def _():
            along(chip - 1 - step, chip, 0, step).wait_recv()
            across(chip - 1 - step, core, 1 + step).start()

        @pl.when(chip + 1 + step < chips)
        def _():
            along(chip + 1 + step, chip, 1, step).wait_recv()
            across(chip + 1 + step, core, 1 + steps + step).start()

    across(chip, core, 0).wait_send()
    across(chip, 1 - core, 0).wait_recv()
    for step in range(steps):
        @pl.when((chip - step >= 0) & (chip + 1 < chips))
        def _():
            along(chip - step, chip + 1, 0, step).wait_send()

        @pl.when((chip + step < chips) & (chip - 1 >= 0))
        def _():
            along(chip + step, chip - 1, 1, step).wait_send()

        @pl.when(chip - 1 - step >= 0)
        def _():
            across(chip - 1 - step, core, 1 + step).wait_send()
            across(chip - 1 - step, 1 - core, 1 + step).wait_recv()

        @pl.when(chip + 1 + step < chips)
        def _():
            across(chip + 1 + step, core, 1 + steps + step).wait_send()
            across(chip + 1 + step, 1 - core, 1 + steps + step).wait_recv()


def filter_kernel(
    slabs, orbs, shape,
    x_ref, pot_ref, own_ref, panel_ref, gram_ref, cross_ref,
    pack, land, pack_back, land_back, pot_land, wide_a, wide_b, level, gath, part, part_land, rows_land,
    a_send, a_recv, p_send, p_recv, b_send, b_recv, c_send, c_recv,
    g_send, g_recv, gs_send, gs_recv, h_send, h_recv, hs_send, hs_recv,
):
    planes, rows_y, rows_z = shape
    points = planes * rows_y * rows_z
    here, me = lax.axis_index("space"), lax.axis_index("orb")
    chunk = points // slabs
    width = LANES // slabs

    barrier = pltpu.get_barrier_semaphore()
    for hop in range(1, slabs):
        pl.semaphore_signal(
            barrier, inc=1, device_id={"space": lax.rem(here + hop, slabs)}, device_id_type=MESH
        )
    for hop in range(1, orbs):
        pl.semaphore_signal(
            barrier, inc=1, device_id={"orb": lax.rem(me + hop, orbs)}, device_id_type=MESH
        )
    pl.semaphore_wait(barrier, slabs - 1 + orbs - 1)

    exchange(slabs, here, p_send, p_recv, lambda there: pot_ref, pot_land)

    def store_pack(j, at, value):
        pack[j, at, :] = value

    regroup(lambda r, at: x_ref[pl.ds(r * chunk + at.start, at.size), :], store_pack, slabs, chunk)
    exchange(slabs, here, a_send, a_recv, lambda there: pack.at[there], land)
    land[here] = pack[here]
    pot_land[here] = pot_ref[...]
    wait_exchange(slabs, here, p_send, p_recv, lambda there: pot_ref, pot_land)

    thin = points // LANES
    lane_group = lax.broadcasted_iota(jnp.int32, (thin, LANES), 1) // width
    fields = [pot_land[s] for s in range(slabs)]
    for l in range(LANES):
        value = None
        for s in range(slabs):
            spread = jnp.broadcast_to(fields[s][:, l : l + 1], (thin, LANES))
            value = spread if value is None else jnp.where(lane_group == s, spread, value)
        level[pl.ds(l * thin, thin), :] = (value - (SHIFT_MID + 1.5 * STENCIL[0])) * (1.0 / HALF_WIDTH)

    wait_exchange(slabs, here, a_send, a_recv, lambda there: pack.at[there], land)

    def put(target, row, value):
        target[pl.ds(points + row, value.shape[0]), :] = value
        target[pl.ds(row, value.shape[0]), :] = pltpu.roll(value, width, 1)
        target[pl.ds(2 * points + row, value.shape[0]), :] = pltpu.roll(value, LANES - width, 1)

    regroup(
        lambda r, at: land[r, at, :],
        lambda j, at, value: put(wide_a, j * chunk + at.start, value),
        slabs, chunk,
    )

    plane = rows_y * rows_z
    taps = [-0.5 * c / HALF_WIDTH for c in STENCIL]

    def sweep(source, target, first):
        def body(y, carry):
            for p in range(planes):
                def line(q, yy):
                    return source[pl.ds(pl.multiple_of(points + q * plane + yy * rows_z, rows_z), rows_z), :]

                row = pl.multiple_of(p * plane + y * rows_z, rows_z)
                centre = line(p, y)
                total = level[pl.ds(row, rows_z), :] * centre
                for m in range(1, REACH + 1):
                    near = line(p + m, y) + line(p - m, y)
                    near += line(p, lax.rem(y + m, rows_y)) + line(p, lax.rem(y + rows_y - m, rows_y))
                    near += pltpu.roll(centre, m, 0) + pltpu.roll(centre, rows_z - m, 0)
                    total += taps[m] * near
                if not first:
                    before = target[pl.ds(pl.multiple_of(points + row, rows_z), rows_z), :]
                    total = 2.0 * total - before
                put(target, row, total)
            return carry

        lax.fori_loop(0, rows_y, body, 0)

    sweep(wide_a, wide_b, True)
    source, target = wide_b, wide_a
    for _ in range(DEGREE - 1):
        sweep(source, target, False)
        source, target = target, source

    def store_back(j, at, value):
        pack_back[j, at, :] = value

    regroup(
        lambda r, at: source[pl.ds(points + r * chunk + at.start, at.size), :], store_back, slabs, chunk
    )
    exchange(slabs, here, b_send, b_recv, lambda there: pack_back.at[there], land_back)
    land_back[here] = pack_back[here]
    wait_exchange(slabs, here, b_send, b_recv, lambda there: pack_back.at[there], land_back)

    def store_own(j, at, value):
        own_ref[pl.ds(j * chunk + at.start, at.size), :] = value

    regroup(lambda r, at: land_back[r, at, :], store_own, slabs, chunk)

    panel_dev = PANEL // orbs
    folds = LANES // panel_dev
    fold = points // folds
    step = min(fold, 32)
    fold_group = lax.broadcasted_iota(jnp.int32, (step, LANES), 1) // panel_dev

    def folded(block, carry):
        at = pl.multiple_of(block * step, step)
        out = None
        for r in range(folds):
            piece = own_ref[pl.ds(r * fold + at, step), :]
            piece = pltpu.roll(piece, r * panel_dev, 1) if r else piece
            out = piece if out is None else jnp.where(fold_group == r, piece, out)
        gath[me, pl.ds(at, step), :] = out
        return carry

    lax.fori_loop(0, fold // step, folded, 0)
    gather_orb(orbs, me, gath, g_send, g_recv, gs_send, gs_recv)

    for tile in range(PANEL // LANES):
        def store_panel(j, at, value):
            panel_ref[pl.ds(j * fold + at.start, at.size), tile * LANES : (tile + 1) * LANES] = value

        regroup(lambda r, at: gath[tile * folds + r, at, :], store_panel, folds, fold)

    part[...] = jnp.zeros_like(part)
    block = 512

    def product(k, carry):
        at = pl.ds(pl.multiple_of(k * block, block), block)
        part[...] += dot(own_ref[at, :], panel_ref[at, :], (0, 0))
        return carry

    lax.fori_loop(0, points // block, product, 0)
    exchange(slabs, here, c_send, c_recv, lambda there: part, part_land)
    part_land[here] = part[...]
    wait_exchange(slabs, here, c_send, c_recv, lambda there: part, part_land)
    total = part_land[0]
    for s in range(1, slabs):
        total += part_land[s]
    total = total / (points * slabs)
    cross_ref[...] = total
    rows_land[me] = total[:panel_dev]
    gather_orb(orbs, me, rows_land, h_send, h_recv, hs_send, hs_recv)
    for o in range(orbs):
        gram_ref[o * panel_dev : (o + 1) * panel_dev, :] = rows_land[o]


def block_inverse(a):
    n = LANES
    tiles = n // 8
    rows = lax.broadcasted_iota(jnp.int32, (8, n), 0)
    cols = lax.broadcasted_iota(jnp.int32, (8, n), 1)
    work = [a[8 * t : 8 * t + 8] for t in range(tiles)]
    unit = [jnp.where(rows + 8 * t == cols, 1.0, 0.0).astype(jnp.float32) for t in range(tiles)]
    for j in range(n - 1):
        t0, s = divmod(j, 8)
        pivot = jnp.broadcast_to(work[t0][s : s + 1, j : j + 1], (1, n))
        scale = 1.0 / pivot
        row = jnp.broadcast_to(work[t0][s : s + 1] * scale, (8, n))
        other = jnp.broadcast_to(unit[t0][s : s + 1] * scale, (8, n))
        for t in range(t0, tiles):
            column = jnp.broadcast_to(work[t][:, j : j + 1], (8, n))
            if t == t0:
                column = jnp.where(rows > s, column, 0.0)
            work[t] = work[t] - column * row
            unit[t] = unit[t] - column * other
    out = []
    for t in range(tiles):
        pivots = jnp.sum(jnp.where(rows + 8 * t == cols, work[t], 0.0), axis=1, keepdims=True)
        out.append(unit[t] * (1.0 / jnp.sqrt(pivots)))
    return jnp.concatenate(out, axis=0)


def solve_kernel(orbs, own_ref, panel_ref, gram_ref, cross_ref, out_ref, work, inverse, weights):
    panel_dev = PANEL // orbs
    me = lax.axis_index("orb")
    n = LANES
    blocks = PANEL // n
    work[...] = gram_ref[...]
    inverse[...] = jnp.zeros_like(inverse)

    def factor(b, carry):
        at = pl.multiple_of(b * n, n)
        diag = block_inverse(work[pl.ds(at, n), pl.ds(at, n)])
        inverse[pl.ds(at, n), pl.ds(at, n)] = diag
        for i in range(1, blocks):
            @pl.when(i > b)
            def _():
                work[i * n : (i + 1) * n, pl.ds(at, n)] = dot(
                    work[i * n : (i + 1) * n, pl.ds(at, n)], diag, (1, 1)
                )
        for i in range(1, blocks):
            @pl.when(i > b)
            def _():
                left = work[i * n : (i + 1) * n, pl.ds(at, n)]
                for k in range(1, i + 1):
                    @pl.when(k > b)
                    def _():
                        right = work[k * n : (k + 1) * n, pl.ds(at, n)]
                        work[i * n : (i + 1) * n, k * n : (k + 1) * n] -= dot(left, right, (1, 1))
        return carry

    lax.fori_loop(0, blocks, factor, 0)
    for i in range(1, blocks):
        span = i * n
        inner = dot(work[i * n : (i + 1) * n, :span], inverse[:span, :span], (1, 0))
        inverse[i * n : (i + 1) * n, :span] = -dot(
            inverse[i * n : (i + 1) * n, i * n : (i + 1) * n], inner, (1, 0)
        )

    middle = dot(cross_ref[...], inverse[...], (1, 1))
    weights[...] = -dot(middle, inverse[...], (1, 0))
    weights[:panel_dev, :] = inverse[pl.ds(pl.multiple_of(me * panel_dev, panel_dev), panel_dev), :]
    points = own_ref.shape[0]
    block = 256
    lanes = lax.broadcasted_iota(jnp.int32, (block, LANES), 1)

    def final(k, carry):
        at = pl.ds(pl.multiple_of(k * block, block), block)
        kept = jnp.where(lanes < panel_dev, 0.0, own_ref[at, :])
        out_ref[at, :] = kept + dot(panel_ref[at, :], weights[...], (1, 1))
        return carry

    lax.fori_loop(0, points // block, final, 0)


def per_device(slabs, orbs, orbitals, potential):
    planes, rows_y, rows_z, columns = orbitals.shape
    points = planes * rows_y * rows_z
    panel_dev = PANEL // orbs
    folds = LANES // panel_dev
    thin = points // LANES
    f32 = jnp.float32
    vmem = pl.BlockSpec(memory_space=pltpu.VMEM)
    dma = pltpu.SemaphoreType.DMA
    steps = max(orbs // 2 - 1, 1)
    flat = orbitals.reshape(points, columns)
    own, panel, gram, cross = pl.pallas_call(
        functools.partial(filter_kernel, slabs, orbs, (planes, rows_y, rows_z)),
        out_shape=[
            jax.ShapeDtypeStruct((points, LANES), f32),
            jax.ShapeDtypeStruct((points, PANEL), f32),
            jax.ShapeDtypeStruct((PANEL, PANEL), f32),
            jax.ShapeDtypeStruct((LANES, PANEL), f32),
        ],
        in_specs=[vmem] * 2,
        out_specs=[vmem] * 4,
        scratch_shapes=[pltpu.VMEM((slabs, points // slabs, LANES), f32)] * 4
        + [
            pltpu.VMEM((slabs, thin, LANES), f32),
            pltpu.VMEM((3 * points, LANES), f32),
            pltpu.VMEM((3 * points, LANES), f32),
            pltpu.VMEM((points, LANES), f32),
            pltpu.VMEM((orbs, points // folds, LANES), f32),
            pltpu.VMEM((LANES, PANEL), f32),
            pltpu.VMEM((slabs, LANES, PANEL), f32),
            pltpu.VMEM((orbs, panel_dev, PANEL), f32),
        ]
        + [dma((slabs,))] * 8
        + [dma((2, steps))] * 2 + [dma((2 * steps + 1,))] * 2
        + [dma((2, steps))] * 2 + [dma((2 * steps + 1,))] * 2,
        compiler_params=pltpu.CompilerParams(
            collective_id=0, has_side_effects=True, vmem_limit_bytes=48 << 20
        ),
    )(flat, potential.reshape(LANES, thin).T)
    out = pl.pallas_call(
        functools.partial(solve_kernel, orbs),
        out_shape=jax.ShapeDtypeStruct((points, LANES), f32),
        in_specs=[vmem] * 4,
        out_specs=vmem,
        scratch_shapes=[
            pltpu.VMEM((PANEL, PANEL), f32),
            pltpu.VMEM((PANEL, PANEL), f32),
            pltpu.VMEM((LANES, PANEL), f32),
        ],
        compiler_params=pltpu.CompilerParams(vmem_limit_bytes=32 << 20),
    )(own, panel, gram, cross)
    return out.reshape(planes, rows_y, rows_z, columns)


def solution(mesh):
    placed = (P("space", None, None, "orb"), P("space", None, None))
    return jax.shard_map(
        functools.partial(per_device, mesh.shape["space"], mesh.shape["orb"]),
        mesh=mesh,
        in_specs=placed,
        out_specs=P("space", None, None, "orb"),
        check_vma=False,
    )
```

time: 522 us -> 190 us (0.36); the launches traced: 515 us -> 190 us
  waiting for transfers between devices: 252 us -> 0 us
  Pallas kernels: 0 us -> 185 us
  other arithmetic: 152 us -> 0 us
  local copies, waits for them, and re-layouts: 54.5 us -> 4.31 us
  matrix products: 29 us -> 0 us
  between operations: 17 us -> 0.02 us
  starting transfers between devices: 10.5 us -> 0 us
    pallas_call x0 -> x2, Pallas kernels: none -> 185 us  [the longest x1 129 us: per_device(): pl.pallas_call(functools.partial(filter_kernel, slabs, orbs, (planes, row...]
    ppermute x8 -> x0, waiting for transfers between devices: 153 us -> none  [the longest x4 79.4 us: padded_2(): after = lax.ppermute(leading, axis, down)]
    another operation x18 -> x0, other arithmetic: 123 us -> none  [the longest x14 82.5 us: per_device(): lower_factor = jnp.linalg.cholesky(gram_full)]
    psum x1 -> x0, waiting for transfers between devices: 51 us -> none  [per_device(): gram_full, coupling = lax.psum((gram_part, coupling_part), 'space')]
    all_gather x1 -> x0, waiting for transfers between devices: 47.5 us -> none  [per_device(): panel = lax.all_gather(panel_own, 'orb', axis=1, tiled=True)]
    slice x66 -> x0, local copies, waits for them, and re-layouts: 37.4 us -> none  [the longest x64 35.9 us: hamilton(): jnp.roll(field, offset, axis) + jnp.roll(field, -offset, axis)]
    dot_general x6 -> x0, matrix products: 23.3 us -> none  [the longest x1 10.7 us: per_device(): gram_part = jnp.dot(panel.T, panel, precision=highest)]
    sub x3 -> x0, other arithmetic: 20.7 us -> none  [chebyshev(): 2.0 * (hamilton(current, potential) - SHIFT_MID * current) / HALF_WIDTH]
  transfers between devices with their start and end apart: 10 -> 0, of which waited for: 10 -> 0; matrix products, arithmetic and copies ran while one was open for 5% -> 0% of each run, Pallas kernels for 0% -> 0%
where the time goes in v1:
time: 190 us
  Pallas kernels  185 us (97%)
  local copies, waits for them, and re-layouts  4.31 us (2%)
    pallas_call x1, Pallas kernels, per_device(): pl.pallas_call(functools.partial(filter_kernel, slabs, orbs, (planes, row...  129 us
    pallas_call x1, Pallas kernels, per_device(): pl.pallas_call(functools.partial(solve_kernel, orbs), out_shape=jax.Shape...  56.2 us

profile of v1, /device:TPU:0, one launch (start us, length us, event | category | flops | bytes accessed | tf_op | source)
XLA Modules:
  0.0 189.7 jit_solution(18244512483527888711)
XLA Ops:
  0.0 0.8 reshape.10
  0.8 0.1 copy.3
  0.9 0.0 copy-start.1
  0.9 1.2 copy-done.1
  2.1 129.2 %shard_map.28 = (f32[2048,128]{1,0:T(8,128)S(1)}, f32[2048,512]{1,0:T(8,128)}, f32[512,512]{1,0:T(8,128)S(1)}, f32[128,512]{1,0:T(8,128)S(1)}) custom-call(f32[2048,128]{1,0:T(8,128)S(1)} %bitcast.3, f32[16,128]{1,0:T(8,128)S(1)} %bitcast.4), custom_call_target="tpu_custom_call" | custom-call | tf_op jit(solution)/shard_map/pallas_call | solution.py:393
  131.3 0.0 copy-start
  131.3 2.2 %copy-done = f32[2048,512]{1,0:T(8,128)S(1)} copy-done((f32[2048,512]{1,0:T(8,128)S(1)}, f32[2048,512]{1,0:T(8,128)}, u32[]{:S(2)}) %copy-start) | copy-done | bytes 4194328
  133.5 56.2 %shard_map.29 = f32[2048,128]{1,0:T(8,128)} custom-call(f32[2048,128]{1,0:T(8,128)S(1)} %get-tuple-element.9.own_ref, f32[2048,512]{1,0:T(8,128)S(1)} %copy-done, f32[512,512]{1,0:T(8,128)S(1)} %get-tuple-element.11.gram_ref, f32[128,512]{1,0:T(8,128)S(1)} %get-tuple-element.12.cross_ref), custom_call_target="tpu_custom_call" | custom-call | tf_op jit(solution)/shard_map/pallas_call | solution.py:421
Async XLA Ops:
  0.9 1.2 copy-start.1
  131.3 2.2 %copy-start = (f32[2048,512]{1,0:T(8,128)S(1)}, f32[2048,512]{1,0:T(8,128)}, u32[]{:S(2)}) copy-start(f32[2048,512]{1,0:T(8,128)} %get-tuple-element.10.panel_ref) | copy-start | bytes 12582916

commit v2 on v1

--- a/solution.py
+++ b/solution.py
@@ -76,7 +76,7 @@
         ).wait()
 
 
-def gather_orb(count, me, buf, send_sem, recv_sem, side_send, side_recv):
+def gather_orb(count, me, buf, send_sem, recv_sem, side_send, side_recv, arrived=lambda chip: None):
     chips = count // 2
     chip, core = me // 2, lax.rem(me, 2)
     partner = chip * 2 + (1 - core)
@@ -104,6 +104,18 @@
         )
 
     steps = chips - 1
+
+    def finish(step):
+        @pl.when(chip - 1 - step >= 0)
+        def _():
+            across(chip - 1 - step, 1 - core, 1 + step).wait_recv()
+            arrived(chip - 1 - step)
+
+        @pl.when(chip + 1 + step < chips)
+        def _():
+            across(chip + 1 + step, 1 - core, 1 + steps + step).wait_recv()
+            arrived(chip + 1 + step)
+
     for step in range(steps):
         @pl.when((chip - step >= 0) & (chip + 1 < chips))
         def _():
@@ -115,6 +127,10 @@
 
         if step == 0:
             across(chip, core, 0).start()
+            across(chip, 1 - core, 0).wait_recv()
+            arrived(chip)
+        else:
+            finish(step - 1)
 
         @pl.when(chip - 1 - step >= 0)
         def _():
@@ -126,8 +142,8 @@
             along(chip + 1 + step, chip, 1, step).wait_recv()
             across(chip + 1 + step, core, 1 + steps + step).start()
 
+    finish(steps - 1)
     across(chip, core, 0).wait_send()
-    across(chip, 1 - core, 0).wait_recv()
     for step in range(steps):
         @pl.when((chip - step >= 0) & (chip + 1 < chips))
         def _():
@@ -140,19 +156,17 @@
         @pl.when(chip - 1 - step >= 0)
         def _():
             across(chip - 1 - step, core, 1 + step).wait_send()
-            across(chip - 1 - step, 1 - core, 1 + step).wait_recv()
 
         @pl.when(chip + 1 + step < chips)
         def _():
             across(chip + 1 + step, core, 1 + steps + step).wait_send()
-            across(chip + 1 + step, 1 - core, 1 + steps + step).wait_recv()
 
 
 def filter_kernel(
     slabs, orbs, shape,
     x_ref, pot_ref, own_ref, panel_ref, gram_ref, cross_ref,
     pack, land, pack_back, land_back, pot_land, wide_a, wide_b, level, gath, part, part_land, rows_land,
-    a_send, a_recv, p_send, p_recv, b_send, b_recv, c_send, c_recv,
+    a_send, a_recv, p_send, p_recv, b_send, b_recv, c_send, c_recv, d_send, d_recv,
     g_send, g_recv, gs_send, gs_recv, h_send, h_recv, hs_send, hs_recv,
 ):
     planes, rows_y, rows_z = shape
@@ -269,33 +283,55 @@
         return carry
 
     lax.fori_loop(0, fold // step, folded, 0)
-    gather_orb(orbs, me, gath, g_send, g_recv, gs_send, gs_recv)
-
-    for tile in range(PANEL // LANES):
+
+    block = 512
+
+    def take(tile):
+        lanes = pl.ds(pl.multiple_of(tile * LANES, LANES), LANES)
+
         def store_panel(j, at, value):
-            panel_ref[pl.ds(j * fold + at.start, at.size), tile * LANES : (tile + 1) * LANES] = value
+            panel_ref[pl.ds(j * fold + at.start, at.size), lanes] = value
 
         regroup(lambda r, at: gath[tile * folds + r, at, :], store_panel, folds, fold)
 
-    part[...] = jnp.zeros_like(part)
-    block = 512
-
-    def product(k, carry):
-        at = pl.ds(pl.multiple_of(k * block, block), block)
-        part[...] += dot(own_ref[at, :], panel_ref[at, :], (0, 0))
-        return carry
-
-    lax.fori_loop(0, points // block, product, 0)
-    exchange(slabs, here, c_send, c_recv, lambda there: part, part_land)
+        def product(k, total):
+            at = pl.ds(pl.multiple_of(k * block, block), block)
+            return total + dot(own_ref[at, :], panel_ref[at, lanes], (0, 0))
+
+        part[:, lanes] = lax.fori_loop(
+            0, points // block, product, jnp.zeros((LANES, LANES), jnp.float32)
+        )
+
+    if folds == 2:
+        gather_orb(orbs, me, gath, g_send, g_recv, gs_send, gs_recv, take)
+    else:
+        gather_orb(orbs, me, gath, g_send, g_recv, gs_send, gs_recv)
+
+        def each(tile, carry):
+            take(tile)
+            return carry
+
+        lax.fori_loop(0, PANEL // LANES, each, 0)
+
+    top, rest = part.at[:panel_dev], part.at[panel_dev:]
+    top_land, rest_land = part_land.at[:, :panel_dev], part_land.at[:, panel_dev:]
+    exchange(slabs, here, c_send, c_recv, lambda there: top, top_land)
+    exchange(slabs, here, d_send, d_recv, lambda there: rest, rest_land)
     part_land[here] = part[...]
-    wait_exchange(slabs, here, c_send, c_recv, lambda there: part, part_land)
-    total = part_land[0]
-    for s in range(1, slabs):
-        total += part_land[s]
-    total = total / (points * slabs)
-    cross_ref[...] = total
-    rows_land[me] = total[:panel_dev]
+    points_all = points * slabs
+
+    def summed(view):
+        total = view[0]
+        for s in range(1, slabs):
+            total += view[s]
+        return total / points_all
+
+    wait_exchange(slabs, here, c_send, c_recv, lambda there: top, top_land)
+    rows_land[me] = summed(top_land)
     gather_orb(orbs, me, rows_land, h_send, h_recv, hs_send, hs_recv)
+    wait_exchange(slabs, here, d_send, d_recv, lambda there: rest, rest_land)
+    cross_ref[:panel_dev, :] = jnp.zeros((panel_dev, PANEL), jnp.float32)
+    cross_ref[panel_dev:, :] = summed(rest_land)
     for o in range(orbs):
         gram_ref[o * panel_dev : (o + 1) * panel_dev, :] = rows_land[o]
 
@@ -307,18 +343,55 @@
     cols = lax.broadcasted_iota(jnp.int32, (8, n), 1)
     work = [a[8 * t : 8 * t + 8] for t in range(tiles)]
     unit = [jnp.where(rows + 8 * t == cols, 1.0, 0.0).astype(jnp.float32) for t in range(tiles)]
-    for j in range(n - 1):
-        t0, s = divmod(j, 8)
-        pivot = jnp.broadcast_to(work[t0][s : s + 1, j : j + 1], (1, n))
-        scale = 1.0 / pivot
-        row = jnp.broadcast_to(work[t0][s : s + 1] * scale, (8, n))
-        other = jnp.broadcast_to(unit[t0][s : s + 1] * scale, (8, n))
-        for t in range(t0, tiles):
-            column = jnp.broadcast_to(work[t][:, j : j + 1], (8, n))
-            if t == t0:
-                column = jnp.where(rows > s, column, 0.0)
-            work[t] = work[t] - column * row
-            unit[t] = unit[t] - column * other
+    for t0 in range(tiles):
+        base = 8 * t0
+        columns = [jnp.broadcast_to(work[t0][:, base + k : base + k + 1], (8, n)) for k in range(8)]
+        small = {
+            (i, k): jnp.broadcast_to(columns[k][i : i + 1], (8, n)) for i in range(8) for k in range(i + 1)
+        }
+        lower, scales = {}, []
+        for j in range(8):
+            scales.append(1.0 / small[j, j])
+            for i in range(j + 1, 8):
+                lower[i, j] = small[i, j] * scales[j]
+            for i in range(j + 1, 8):
+                for k in range(j + 1, i + 1):
+                    small[i, k] = small[i, k] - lower[i, j] * small[k, j]
+        turned = {}
+        for j in range(8):
+            for i in range(j + 1, 8):
+                value = lower[i, j]
+                for k in range(j + 1, i):
+                    value = value + lower[i, k] * turned[k, j]
+                turned[i, j] = -value
+        a_row, u_row = work[t0], unit[t0]
+        a_new, u_new = a_row, u_row
+        for k in range(7):
+            weight = jnp.zeros((8, n), jnp.float32)
+            for i in range(k + 1, 8):
+                weight = jnp.where(rows == i, turned[i, k], weight)
+            a_new = a_new + weight * jnp.broadcast_to(a_row[k : k + 1], (8, n))
+            u_new = u_new + weight * jnp.broadcast_to(u_row[k : k + 1], (8, n))
+        work[t0], unit[t0] = a_new, u_new
+        if t0 == tiles - 1:
+            break
+        a_out = u_out = None
+        for i in range(8):
+            weight = jnp.where(rows == i, scales[i], 0.0)
+            for k in range(i):
+                weight = jnp.where(rows == k, turned[i, k] * scales[i], weight)
+            a_term = weight * jnp.broadcast_to(a_new[i : i + 1], (8, n))
+            u_term = weight * jnp.broadcast_to(u_new[i : i + 1], (8, n))
+            a_out = a_term if a_out is None else a_out + a_term
+            u_out = u_term if u_out is None else u_out + u_term
+        a_rows = [jnp.broadcast_to(a_out[k : k + 1], (8, n)) for k in range(8)]
+        u_rows = [jnp.broadcast_to(u_out[k : k + 1], (8, n)) for k in range(8)]
+        for t in range(t0 + 1, tiles):
+            before = work[t]
+            for k in range(8):
+                column = jnp.broadcast_to(before[:, base + k : base + k + 1], (8, n))
+                work[t] = work[t] - column * a_rows[k]
+                unit[t] = unit[t] - column * u_rows[k]
     out = []
     for t in range(tiles):
         pivots = jnp.sum(jnp.where(rows + 8 * t == cols, work[t], 0.0), axis=1, keepdims=True)
@@ -411,7 +484,7 @@
             pltpu.VMEM((slabs, LANES, PANEL), f32),
             pltpu.VMEM((orbs, panel_dev, PANEL), f32),
         ]
-        + [dma((slabs,))] * 8
+        + [dma((slabs,))] * 10
         + [dma((2, steps))] * 2 + [dma((2 * steps + 1,))] * 2
         + [dma((2, steps))] * 2 + [dma((2 * steps + 1,))] * 2,
         compiler_params=pltpu.CompilerParams(

time: 190 us -> 155 us (0.82)
  Pallas kernels: 185 us -> 150 us
    pallas_call x1, Pallas kernels: 56.2 us -> 32.3 us  [per_device(): pl.pallas_call(functools.partial(solve_kernel, orbs), out_shape=jax.Shape...]
    pallas_call x1, Pallas kernels: 129 us -> 118 us  [per_device(): pl.pallas_call(functools.partial(filter_kernel, slabs, orbs, (planes, row...]
where the time goes in v2:
time: 155 us; the launch traced here: 154 us
  Pallas kernels  150 us (97%)
  local copies, waits for them, and re-layouts  4.31 us (3%)
    pallas_call x1, Pallas kernels, per_device(): pl.pallas_call(functools.partial(filter_kernel, slabs, orbs, (planes, row...  118 us
    pallas_call x1, Pallas kernels, per_device(): pl.pallas_call(functools.partial(solve_kernel, orbs), out_shape=jax.Shape...  32.3 us
    unnamed x4, local copies, waits for them, and re-layouts  3.43 us

profile of v2, /device:TPU:0, one launch (start us, length us, event | category | flops | bytes accessed | tf_op | source)
XLA Modules:
  0.0 154.2 jit_solution(1113163569198857826)
XLA Ops:
  0.0 0.8 reshape.10
  0.8 0.1 copy.3
  0.9 0.0 copy-start.1
  0.9 1.2 copy-done.1
  2.1 117.6 %shard_map.28 = (f32[2048,128]{1,0:T(8,128)S(1)}, f32[2048,512]{1,0:T(8,128)}, f32[512,512]{1,0:T(8,128)S(1)}, f32[128,512]{1,0:T(8,128)S(1)}) custom-call(f32[2048,128]{1,0:T(8,128)S(1)} %bitcast.3, f32[16,128]{1,0:T(8,128)S(1)} %bitcast.4), custom_call_target="tpu_custom_call" | custom-call | tf_op jit(solution)/shard_map/pallas_call | solution.py:466
  119.7 0.0 copy-start
  119.7 2.2 %copy-done = f32[2048,512]{1,0:T(8,128)S(1)} copy-done((f32[2048,512]{1,0:T(8,128)S(1)}, f32[2048,512]{1,0:T(8,128)}, u32[]{:S(2)}) %copy-start) | copy-done | bytes 4194328
  121.9 32.3 %shard_map.29 = f32[2048,128]{1,0:T(8,128)} custom-call(f32[2048,128]{1,0:T(8,128)S(1)} %get-tuple-element.9.own_ref, f32[2048,512]{1,0:T(8,128)S(1)} %copy-done, f32[512,512]{1,0:T(8,128)S(1)} %get-tuple-element.11.gram_ref, f32[128,512]{1,0:T(8,128)S(1)} %get-tuple-element.12.cross_ref), custom_call_target="tpu_custom_call" | custom-call | tf_op jit(solution)/shard_map/pallas_call | solution.py:494
Async XLA Ops:
  0.9 1.2 copy-start.1
  119.7 2.2 %copy-start = (f32[2048,512]{1,0:T(8,128)S(1)}, f32[2048,512]{1,0:T(8,128)}, u32[]{:S(2)}) copy-start(f32[2048,512]{1,0:T(8,128)} %get-tuple-element.10.panel_ref) | copy-start | bytes 12582916

commit v3 on v2

--- a/solution.py
+++ b/solution.py
@@ -76,7 +76,7 @@
         ).wait()
 
 
-def gather_orb(count, me, buf, send_sem, recv_sem, side_send, side_recv, arrived=lambda chip: None):
+def gather_orb(count, me, buf, send_sem, recv_sem, side_send, side_recv, arrived=lambda chip: None, during=None):
     chips = count // 2
     chip, core = me // 2, lax.rem(me, 2)
     partner = chip * 2 + (1 - core)
@@ -127,9 +127,14 @@
 
         if step == 0:
             across(chip, core, 0).start()
+            if during:
+                during[0]()
+        if step == (1 if during else 0):
+            if during:
+                during[1]()
             across(chip, 1 - core, 0).wait_recv()
             arrived(chip)
-        else:
+        if step:
             finish(step - 1)
 
         @pl.when(chip - 1 - step >= 0)
@@ -162,11 +167,162 @@
             across(chip + 1 + step, core, 1 + steps + step).wait_send()
 
 
+def split_filter(
+    slabs, shape, here, me, x_ref, pot_ref, own_ref, pack, land, pack_back, land_back, pot_land,
+    wide_a, wide_b, level, gath, out_sems, pot_sems, back_sems,
+):
+    planes, rows_y, rows_z = shape
+    points = planes * rows_y * rows_z
+    slots = 2 * slabs
+    width = LANES // slots
+    rows = points // slots
+    plane = 3 * rows
+    thin = points // LANES
+    step = 16
+    slot = lax.broadcasted_iota(jnp.int32, (step, LANES), 1) // width
+
+    def merge(parts):
+        out = None
+        for u, (value, v) in enumerate(parts):
+            turn = ((u - v) * width) % LANES
+            value = pltpu.roll(value, turn, 1) if turn else value
+            out = value if out is None else jnp.where(slot == u, value, out)
+        return out
+
+    def over(body):
+        def one(block, carry):
+            body(pl.multiple_of(block * step, step))
+            return carry
+
+        lax.fori_loop(0, rows // step, one, 0)
+
+    def half(buf, h):
+        return buf.at[:, h * rows : (h + 1) * rows]
+
+    def send(buf, landing, h, sems):
+        exchange(slabs, here, *sems[h], lambda there: half(buf, h).at[there], half(landing, h))
+        landing[here, h * rows : (h + 1) * rows] = buf[here, h * rows : (h + 1) * rows]
+
+    def wait(buf, landing, h, sems):
+        wait_exchange(slabs, here, *sems[h], lambda there: half(buf, h).at[there], half(landing, h))
+
+    def pack_half(h):
+        def body(at):
+            parts = [x_ref[pl.ds(q * rows + at, step), :] for q in range(slots)]
+            for j in range(slabs):
+                pack[j, pl.ds(h * rows + at, step), :] = merge([(part, h * slabs + j) for part in parts])
+
+        over(body)
+        send(pack, land, h, out_sems)
+
+    def put(target, p, row, value):
+        odd = lax.rem(lax.broadcasted_iota(jnp.int32, value.shape, 1) // width, 2)
+        size = value.shape[0]
+        swapped = jnp.where(odd == 0, pltpu.roll(value, LANES - width, 1), pltpu.roll(value, width, 1))
+        target[pl.ds((planes + p) * plane + rows + row, size), :] = value
+        target[pl.ds((planes + p) * plane + row, size), :] = swapped
+        target[pl.ds((planes + p) * plane + 2 * rows + row, size), :] = swapped
+        target[pl.ds(p * plane + rows + row, size), :] = pltpu.roll(value, 2 * width, 1)
+        target[pl.ds((2 * planes + p) * plane + rows + row, size), :] = pltpu.roll(value, LANES - 2 * width, 1)
+
+    taps = [-0.5 * c / HALF_WIDTH for c in STENCIL]
+
+    def sweep(source, target, first):
+        def body(y, carry):
+            for p in range(planes):
+                def line(q, yy):
+                    row = pl.multiple_of((planes + q) * plane + rows + yy * rows_z, rows_z)
+                    return source[pl.ds(row, rows_z), :]
+
+                row = pl.multiple_of(y * rows_z, rows_z)
+                centre = line(p, y)
+                total = level[pl.ds(p * rows + row, rows_z), :] * centre
+                for m in range(1, REACH + 1):
+                    near = line(p + m, y) + line(p - m, y) + line(p, y + m) + line(p, y - m)
+                    near += pltpu.roll(centre, m, 0) + pltpu.roll(centre, rows_z - m, 0)
+                    total += taps[m] * near
+                if not first:
+                    total = 2.0 * total - target[pl.ds((planes + p) * plane + rows + row, rows_z), :]
+                put(target, p, row, total)
+            return carry
+
+        lax.fori_loop(0, rows_y // 2, body, 0)
+
+    def filter_half(h):
+        wait(pack, land, h, out_sems)
+
+        def unpack(at):
+            parts = [land[i, pl.ds(h * rows + at, step), :] for i in range(slabs)]
+            for p in range(planes):
+                put(wide_a, p, at, merge([(parts[u // 2], 2 * p + u % 2) for u in range(slots)]))
+
+        over(unpack)
+        sweep(wide_a, wide_b, True)
+        source, target = wide_b, wide_a
+        for _ in range(DEGREE - 1):
+            sweep(source, target, False)
+            source, target = target, source
+
+        def body(at):
+            parts = [source[pl.ds((planes + p) * plane + rows + at, step), :] for p in range(planes)]
+            for i in range(slabs):
+                pack_back[i, pl.ds(h * rows + at, step), :] = merge(
+                    [(parts[q // 2], 2 * i + q % 2) for q in range(slots)]
+                )
+
+        over(body)
+        send(pack_back, land_back, h, back_sems)
+
+    pack_half(0)
+    pack_half(1)
+    pot_land[here] = pot_ref[...]
+    wait_exchange(slabs, here, *pot_sems, lambda there: pot_ref, pot_land)
+    lane_slot = lax.broadcasted_iota(jnp.int32, (thin, LANES), 1) // width
+    fields = [pot_land[s] for s in range(slabs)]
+    pieces = rows // thin
+    for p in range(planes):
+        for e in range(pieces):
+            value = None
+            for u in range(slots):
+                l = (2 * p + u % 2) * pieces + e
+                spread = jnp.broadcast_to(fields[u // 2][:, l : l + 1], (thin, LANES))
+                value = spread if value is None else jnp.where(lane_slot == u, spread, value)
+            level[pl.ds(p * rows + e * thin, thin), :] = (
+                value - (SHIFT_MID + 1.5 * STENCIL[0])
+            ) * (1.0 / HALF_WIDTH)
+
+    filter_half(0)
+    wait(pack_back, land_back, 0, back_sems)
+
+    def fold_own(at):
+        parts = [land_back[j, pl.ds(at, step), :] for j in range(slabs)]
+        for k in range(slabs):
+            gath[me, pl.ds(k * rows + at, step), :] = merge(
+                [(parts[u % slabs], (u // slabs) * slabs + k) for u in range(slots)]
+            )
+
+    over(fold_own)
+
+    def finish():
+        wait(pack_back, land_back, 1, back_sems)
+
+        def body(at):
+            parts = [
+                land_back[u % slabs, pl.ds((u // slabs) * rows + at, step), :] for u in range(slots)
+            ]
+            for q in range(slots):
+                own_ref[pl.ds(q * rows + at, step), :] = merge([(part, q) for part in parts])
+
+        over(body)
+
+    return (lambda: filter_half(1)), finish
+
+
 def filter_kernel(
-    slabs, orbs, shape,
+    slabs, orbs, shape, split,
     x_ref, pot_ref, own_ref, panel_ref, gram_ref, cross_ref,
     pack, land, pack_back, land_back, pot_land, wide_a, wide_b, level, gath, part, part_land, rows_land,
-    a_send, a_recv, p_send, p_recv, b_send, b_recv, c_send, c_recv, d_send, d_recv,
+    a_send, a_recv, p_send, p_recv, b_send, b_recv, c_send, c_recv, d_send, d_recv, e_send, e_recv, f_send, f_recv,
     g_send, g_recv, gs_send, gs_recv, h_send, h_recv, hs_send, hs_recv,
 ):
     planes, rows_y, rows_z = shape
@@ -188,101 +344,109 @@
 
     exchange(slabs, here, p_send, p_recv, lambda there: pot_ref, pot_land)
 
-    def store_pack(j, at, value):
-        pack[j, at, :] = value
-
-    regroup(lambda r, at: x_ref[pl.ds(r * chunk + at.start, at.size), :], store_pack, slabs, chunk)
-    exchange(slabs, here, a_send, a_recv, lambda there: pack.at[there], land)
-    land[here] = pack[here]
-    pot_land[here] = pot_ref[...]
-    wait_exchange(slabs, here, p_send, p_recv, lambda there: pot_ref, pot_land)
-
-    thin = points // LANES
-    lane_group = lax.broadcasted_iota(jnp.int32, (thin, LANES), 1) // width
-    fields = [pot_land[s] for s in range(slabs)]
-    for l in range(LANES):
-        value = None
-        for s in range(slabs):
-            spread = jnp.broadcast_to(fields[s][:, l : l + 1], (thin, LANES))
-            value = spread if value is None else jnp.where(lane_group == s, spread, value)
-        level[pl.ds(l * thin, thin), :] = (value - (SHIFT_MID + 1.5 * STENCIL[0])) * (1.0 / HALF_WIDTH)
-
-    wait_exchange(slabs, here, a_send, a_recv, lambda there: pack.at[there], land)
-
-    def put(target, row, value):
-        target[pl.ds(points + row, value.shape[0]), :] = value
-        target[pl.ds(row, value.shape[0]), :] = pltpu.roll(value, width, 1)
-        target[pl.ds(2 * points + row, value.shape[0]), :] = pltpu.roll(value, LANES - width, 1)
-
-    regroup(
-        lambda r, at: land[r, at, :],
-        lambda j, at, value: put(wide_a, j * chunk + at.start, value),
-        slabs, chunk,
-    )
-
-    plane = rows_y * rows_z
-    taps = [-0.5 * c / HALF_WIDTH for c in STENCIL]
-
-    def sweep(source, target, first):
-        def body(y, carry):
-            for p in range(planes):
-                def line(q, yy):
-                    return source[pl.ds(pl.multiple_of(points + q * plane + yy * rows_z, rows_z), rows_z), :]
-
-                row = pl.multiple_of(p * plane + y * rows_z, rows_z)
-                centre = line(p, y)
-                total = level[pl.ds(row, rows_z), :] * centre
-                for m in range(1, REACH + 1):
-                    near = line(p + m, y) + line(p - m, y)
-                    near += line(p, lax.rem(y + m, rows_y)) + line(p, lax.rem(y + rows_y - m, rows_y))
-                    near += pltpu.roll(centre, m, 0) + pltpu.roll(centre, rows_z - m, 0)
-                    total += taps[m] * near
-                if not first:
-                    before = target[pl.ds(pl.multiple_of(points + row, rows_z), rows_z), :]
-                    total = 2.0 * total - before
-                put(target, row, total)
-            return carry
-
-        lax.fori_loop(0, rows_y, body, 0)
-
-    sweep(wide_a, wide_b, True)
-    source, target = wide_b, wide_a
-    for _ in range(DEGREE - 1):
-        sweep(source, target, False)
-        source, target = target, source
-
-    def store_back(j, at, value):
-        pack_back[j, at, :] = value
-
-    regroup(
-        lambda r, at: source[pl.ds(points + r * chunk + at.start, at.size), :], store_back, slabs, chunk
-    )
-    exchange(slabs, here, b_send, b_recv, lambda there: pack_back.at[there], land_back)
-    land_back[here] = pack_back[here]
-    wait_exchange(slabs, here, b_send, b_recv, lambda there: pack_back.at[there], land_back)
-
-    def store_own(j, at, value):
-        own_ref[pl.ds(j * chunk + at.start, at.size), :] = value
-
-    regroup(lambda r, at: land_back[r, at, :], store_own, slabs, chunk)
-
     panel_dev = PANEL // orbs
     folds = LANES // panel_dev
     fold = points // folds
-    step = min(fold, 32)
-    fold_group = lax.broadcasted_iota(jnp.int32, (step, LANES), 1) // panel_dev
-
-    def folded(block, carry):
-        at = pl.multiple_of(block * step, step)
-        out = None
-        for r in range(folds):
-            piece = own_ref[pl.ds(r * fold + at, step), :]
-            piece = pltpu.roll(piece, r * panel_dev, 1) if r else piece
-            out = piece if out is None else jnp.where(fold_group == r, piece, out)
-        gath[me, pl.ds(at, step), :] = out
-        return carry
-
-    lax.fori_loop(0, fold // step, folded, 0)
+    during = None
+    if split:
+        during = split_filter(
+            slabs, shape, here, me, x_ref, pot_ref, own_ref, pack, land, pack_back, land_back, pot_land,
+            wide_a, wide_b, level, gath,
+            ((a_send, a_recv), (e_send, e_recv)), (p_send, p_recv), ((b_send, b_recv), (f_send, f_recv)),
+        )
+    else:
+        def store_pack(j, at, value):
+            pack[j, at, :] = value
+
+        regroup(lambda r, at: x_ref[pl.ds(r * chunk + at.start, at.size), :], store_pack, slabs, chunk)
+        exchange(slabs, here, a_send, a_recv, lambda there: pack.at[there], land)
+        land[here] = pack[here]
+        pot_land[here] = pot_ref[...]
+        wait_exchange(slabs, here, p_send, p_recv, lambda there: pot_ref, pot_land)
+
+        thin = points // LANES
+        lane_group = lax.broadcasted_iota(jnp.int32, (thin, LANES), 1) // width
+        fields = [pot_land[s] for s in range(slabs)]
+        for l in range(LANES):
+            value = None
+            for s in range(slabs):
+                spread = jnp.broadcast_to(fields[s][:, l : l + 1], (thin, LANES))
+                value = spread if value is None else jnp.where(lane_group == s, spread, value)
+            level[pl.ds(l * thin, thin), :] = (value - (SHIFT_MID + 1.5 * STENCIL[0])) * (1.0 / HALF_WIDTH)
+
+        wait_exchange(slabs, here, a_send, a_recv, lambda there: pack.at[there], land)
+
+        def put(target, row, value):
+            target[pl.ds(points + row, value.shape[0]), :] = value
+            target[pl.ds(row, value.shape[0]), :] = pltpu.roll(value, width, 1)
+            target[pl.ds(2 * points + row, value.shape[0]), :] = pltpu.roll(value, LANES - width, 1)
+
+        regroup(
+            lambda r, at: land[r, at, :],
+            lambda j, at, value: put(wide_a, j * chunk + at.start, value),
+            slabs, chunk,
+        )
+
+        plane = rows_y * rows_z
+        taps = [-0.5 * c / HALF_WIDTH for c in STENCIL]
+
+        def sweep(source, target, first):
+            def body(y, carry):
+                for p in range(planes):
+                    def line(q, yy):
+                        return source[pl.ds(pl.multiple_of(points + q * plane + yy * rows_z, rows_z), rows_z), :]
+
+                    row = pl.multiple_of(p * plane + y * rows_z, rows_z)
+                    centre = line(p, y)
+                    total = level[pl.ds(row, rows_z), :] * centre
+                    for m in range(1, REACH + 1):
+                        near = line(p + m, y) + line(p - m, y)
+                        near += line(p, lax.rem(y + m, rows_y)) + line(p, lax.rem(y + rows_y - m, rows_y))
+                        near += pltpu.roll(centre, m, 0) + pltpu.roll(centre, rows_z - m, 0)
+                        total += taps[m] * near
+                    if not first:
+                        before = target[pl.ds(pl.multiple_of(points + row, rows_z), rows_z), :]
+                        total = 2.0 * total - before
+                    put(target, row, total)
+                return carry
+
+            lax.fori_loop(0, rows_y, body, 0)
+
+        sweep(wide_a, wide_b, True)
+        source, target = wide_b, wide_a
+        for _ in range(DEGREE - 1):
+            sweep(source, target, False)
+            source, target = target, source
+
+        def store_back(j, at, value):
+            pack_back[j, at, :] = value
+
+        regroup(
+            lambda r, at: source[pl.ds(points + r * chunk + at.start, at.size), :], store_back, slabs, chunk
+        )
+        exchange(slabs, here, b_send, b_recv, lambda there: pack_back.at[there], land_back)
+        land_back[here] = pack_back[here]
+        wait_exchange(slabs, here, b_send, b_recv, lambda there: pack_back.at[there], land_back)
+
+        def store_own(j, at, value):
+            own_ref[pl.ds(j * chunk + at.start, at.size), :] = value
+
+        regroup(lambda r, at: land_back[r, at, :], store_own, slabs, chunk)
+
+        step = min(fold, 32)
+        fold_group = lax.broadcasted_iota(jnp.int32, (step, LANES), 1) // panel_dev
+
+        def folded(block, carry):
+            at = pl.multiple_of(block * step, step)
+            out = None
+            for r in range(folds):
+                piece = own_ref[pl.ds(r * fold + at, step), :]
+                piece = pltpu.roll(piece, r * panel_dev, 1) if r else piece
+                out = piece if out is None else jnp.where(fold_group == r, piece, out)
+            gath[me, pl.ds(at, step), :] = out
+            return carry
+
+        lax.fori_loop(0, fold // step, folded, 0)
 
     block = 512
 
@@ -303,7 +467,7 @@
         )
 
     if folds == 2:
-        gather_orb(orbs, me, gath, g_send, g_recv, gs_send, gs_recv, take)
+        gather_orb(orbs, me, gath, g_send, g_recv, gs_send, gs_recv, take, during)
     else:
         gather_orb(orbs, me, gath, g_send, g_recv, gs_send, gs_recv)
 
@@ -462,9 +626,10 @@
     vmem = pl.BlockSpec(memory_space=pltpu.VMEM)
     dma = pltpu.SemaphoreType.DMA
     steps = max(orbs // 2 - 1, 1)
+    split = folds == 2 and planes == slabs and rows_y // 2 >= REACH and steps >= 2
     flat = orbitals.reshape(points, columns)
     own, panel, gram, cross = pl.pallas_call(
-        functools.partial(filter_kernel, slabs, orbs, (planes, rows_y, rows_z)),
+        functools.partial(filter_kernel, slabs, orbs, (planes, rows_y, rows_z), split),
         out_shape=[
             jax.ShapeDtypeStruct((points, LANES), f32),
             jax.ShapeDtypeStruct((points, PANEL), f32),
@@ -476,15 +641,15 @@
         scratch_shapes=[pltpu.VMEM((slabs, points // slabs, LANES), f32)] * 4
         + [
             pltpu.VMEM((slabs, thin, LANES), f32),
-            pltpu.VMEM((3 * points, LANES), f32),
-            pltpu.VMEM((3 * points, LANES), f32),
+            pltpu.VMEM(((9 if split else 6) * points // 2, LANES), f32),
+            pltpu.VMEM(((9 if split else 6) * points // 2, LANES), f32),
             pltpu.VMEM((points, LANES), f32),
             pltpu.VMEM((orbs, points // folds, LANES), f32),
             pltpu.VMEM((LANES, PANEL), f32),
             pltpu.VMEM((slabs, LANES, PANEL), f32),
             pltpu.VMEM((orbs, panel_dev, PANEL), f32),
         ]
-        + [dma((slabs,))] * 10
+        + [dma((slabs,))] * 14
         + [dma((2, steps))] * 2 + [dma((2 * steps + 1,))] * 2
         + [dma((2, steps))] * 2 + [dma((2 * steps + 1,))] * 2,
         compiler_params=pltpu.CompilerParams(

time: 155 us -> 143 us (0.923)
  Pallas kernels: 150 us -> 138 us
    pallas_call x1, Pallas kernels: 118 us -> 106 us  [per_device(): pl.pallas_call(functools.partial(filter_kernel, slabs, orbs, (planes, row...]
where the time goes in v3:
time: 143 us
  Pallas kernels  138 us (97%)
  local copies, waits for them, and re-layouts  4.31 us (3%)
    pallas_call x1, Pallas kernels, per_device(): pl.pallas_call(functools.partial(filter_kernel, slabs, orbs, (planes, row...  106 us
    pallas_call x1, Pallas kernels, per_device(): pl.pallas_call(functools.partial(solve_kernel, orbs), out_shape=jax.Shape...  32.3 us
    unnamed x4, local copies, waits for them, and re-layouts  3.43 us

profile of v3, /device:TPU:0, one launch (start us, length us, event | category | flops | bytes accessed | tf_op | source)
XLA Modules:
  0.0 142.7 jit_solution(1520555918597635290)
XLA Ops:
  0.0 0.8 reshape.10
  0.8 0.1 copy.3
  0.9 0.0 copy-start.1
  0.9 1.2 copy-done.1
  2.1 106.1 %shard_map.28 = (f32[2048,128]{1,0:T(8,128)S(1)}, f32[2048,512]{1,0:T(8,128)}, f32[512,512]{1,0:T(8,128)S(1)}, f32[128,512]{1,0:T(8,128)S(1)}) custom-call(f32[2048,128]{1,0:T(8,128)S(1)} %bitcast.3, f32[16,128]{1,0:T(8,128)S(1)} %bitcast.4), custom_call_target="tpu_custom_call" | custom-call | tf_op jit(solution)/shard_map/pallas_call | solution.py:631
  108.2 0.0 copy-start
  108.2 2.2 %copy-done = f32[2048,512]{1,0:T(8,128)S(1)} copy-done((f32[2048,512]{1,0:T(8,128)S(1)}, f32[2048,512]{1,0:T(8,128)}, u32[]{:S(2)}) %copy-start) | copy-done | bytes 4194328
  110.4 32.3 %shard_map.29 = f32[2048,128]{1,0:T(8,128)} custom-call(f32[2048,128]{1,0:T(8,128)S(1)} %get-tuple-element.9.own_ref, f32[2048,512]{1,0:T(8,128)S(1)} %copy-done, f32[512,512]{1,0:T(8,128)S(1)} %get-tuple-element.11.gram_ref, f32[128,512]{1,0:T(8,128)S(1)} %get-tuple-element.12.cross_ref), custom_call_target="tpu_custom_call" | custom-call | tf_op jit(solution)/shard_map/pallas_call | solution.py:659
Async XLA Ops:
  0.9 1.2 copy-start.1
  108.2 2.2 %copy-start = (f32[2048,512]{1,0:T(8,128)S(1)}, f32[2048,512]{1,0:T(8,128)}, u32[]{:S(2)}) copy-start(f32[2048,512]{1,0:T(8,128)} %get-tuple-element.10.panel_ref) | copy-start | bytes 12582916

commit v4 on v3

--- a/solution.py
+++ b/solution.py
@@ -653,7 +653,7 @@
         + [dma((2, steps))] * 2 + [dma((2 * steps + 1,))] * 2
         + [dma((2, steps))] * 2 + [dma((2 * steps + 1,))] * 2,
         compiler_params=pltpu.CompilerParams(
-            collective_id=0, has_side_effects=True, vmem_limit_bytes=48 << 20
+            collective_id=0, has_side_effects=True, vmem_limit_bytes=32 << 20
         ),
     )(flat, potential.reshape(LANES, thin).T)
     out = pl.pallas_call(

time: 143 us -> 139 us (0.972)
  local copies, waits for them, and re-layouts: 4.31 us -> 2.13 us
  Pallas kernels: 138 us -> 136 us
    unnamed x4 -> x2, local copies, waits for them, and re-layouts: 3.43 us -> 1.25 us
    pallas_call x1, Pallas kernels: 106 us -> 104 us  [per_device(): pl.pallas_call(functools.partial(filter_kernel, slabs, orbs, (planes, row...]
where the time goes in v4:
time: 139 us
  Pallas kernels  136 us (98%)
  local copies, waits for them, and re-layouts  2.13 us (2%)
    pallas_call x1, Pallas kernels, per_device(): pl.pallas_call(functools.partial(filter_kernel, slabs, orbs, (planes, row...  104 us
    pallas_call x1, Pallas kernels, per_device(): pl.pallas_call(functools.partial(solve_kernel, orbs), out_shape=jax.Shape...  32.3 us

profile of v4, /device:TPU:0, one launch (start us, length us, event | category | flops | bytes accessed | tf_op | source)
XLA Modules:
  0.0 138.6 jit_solution(16739522170605738368)
XLA Ops:
  0.0 0.8 reshape.10
  0.8 0.1 copy.3
  0.9 0.0 copy-start
  0.9 1.2 copy-done
  2.1 104.2 %shard_map.28 = (f32[2048,128]{1,0:T(8,128)S(1)}, f32[2048,512]{1,0:T(8,128)S(1)}, f32[512,512]{1,0:T(8,128)S(1)}, f32[128,512]{1,0:T(8,128)S(1)}) custom-call(f32[2048,128]{1,0:T(8,128)S(1)} %bitcast.3, f32[16,128]{1,0:T(8,128)S(1)} %bitcast.4), custom_call_target="tpu_custom_call" | custom-call | tf_op jit(solution)/shard_map/pallas_call | solution.py:631
  106.3 32.3 %shard_map.29 = f32[2048,128]{1,0:T(8,128)} custom-call(f32[2048,128]{1,0:T(8,128)S(1)} %get-tuple-element.9.own_ref, f32[2048,512]{1,0:T(8,128)S(1)} %get-tuple-element.10.panel_ref, f32[512,512]{1,0:T(8,128)S(1)} %get-tuple-element.11.gram_ref, f32[128,512]{1,0:T(8,128)S(1)} %get-tuple-element.12.cross_ref), custom_call_target="tpu_custom_call" | custom-call | tf_op jit(solution)/shard_map/pallas_call | solution.py:659
Async XLA Ops:
  0.9 1.2 copy-start
